TPU v7x, 32 devices: a whole 2x2x4 slice. The times are simulated.
32 devices in a mesh: blk: 2 (over x), grid: 16 (over z, y, core).
Axes of the slice: x: 2, y: 2, z: 4, core: 2. Of those that a mesh axis runs over, the one named last changes fastest.
Arguments:
- centers: bfloat16 [4096, 512], P(('blk', 'grid')), as said below
- weights: float32 [4096, 1000], P(('blk', 'grid')), may hold values from -6 to 6
- batch_index: int32 [512], replicated, may hold values from 0 to 4095, as said below
- labels: int32 [512], replicated, may hold values from 0 to 999
- sub_index: int32 [256], P(('blk', 'grid')), may hold values from 0 to 127
- eigvecs: bfloat16 [256, 160], P(('blk', 'grid')), may hold values from -0.375 to 0.375
- scales: float32 [160], replicated, may hold values from 1 to 16
Outputs:
- predictions: bfloat16 [512, 1000], replicated
- center_grad: bfloat16 [4096, 1000], P(('blk', 'grid'))
- sub_increment: float32 [256, 1000], P(('blk', 'grid'))
Inputs may be any that keep to these rules, and one draw needn't show every extreme that they name: Each device's block of 128 centers is named by exactly 512 / 32 entries of batch_index. sub_index: entry i names center (i // 8) * 128 + sub_index[i]. centers: row scales of order one.
All inputs are finite; a program needn't handle non-finite values.
Results may differ from a plain program's by a relative error of at most 0.0011.
The roundings to bfloat16 on the way count: a program that leaves them out, or rounds other values in their place, can miss the bound.
Values may be sent and summed in bfloat16 or wider, within the bound.
A program may use at most 64 MiB of HBM per device.

v0:
```python
import jax
import jax.numpy as jnp
from jax import lax
from jax.sharding import PartitionSpec as P

SOFTEN = 1.0
SPREAD = 4.0


def kernel(left, right):
    left_sq = jnp.sum(jnp.square(left.astype(jnp.float32)), axis=1)
    right_sq = jnp.sum(jnp.square(right.astype(jnp.float32)), axis=1)
    cross = lax.dot_general(
        left, right, (((1,), (1,)), ((), ())), preferred_element_type=jnp.float32
    )
    dist = jnp.sqrt(jnp.maximum(left_sq[:, None] + right_sq[None, :] - 2.0 * cross, 0.0) + SOFTEN)
    return jnp.exp(-dist / SPREAD)


def one_hot(label_rows, classes):
    return (label_rows[:, None] == jnp.arange(classes, dtype=jnp.int32)[None, :]).astype(
        jnp.float32
    )


def local(centers, weights, batch_index, labels, sub_index, eigvecs, scales):
    myself = lax.axis_index(("blk", "grid"))
    held = centers.shape[0]
    classes = weights.shape[1]
    owner = batch_index // held
    within = batch_index % held
    picked = jnp.take(centers, within, axis=0).astype(jnp.float32)
    picked = jnp.where((owner == myself)[:, None], picked, 0.0)
    batch = lax.psum(picked, ("blk", "grid")).astype(jnp.bfloat16)
    kbz = kernel(batch, centers).astype(jnp.bfloat16)
    partial_out = jnp.dot(kbz, weights.astype(jnp.bfloat16), preferred_element_type=jnp.float32)
    total = lax.psum(partial_out, ("blk", "grid"))
    predictions = total.astype(jnp.bfloat16)
    resid = (total - one_hot(labels, classes)).astype(jnp.bfloat16)
    subset_here = jnp.take(centers, sub_index, axis=0)
    sub_rows = lax.all_gather(subset_here, ("blk", "grid"), axis=0, tiled=True)
    vec_rows = lax.all_gather(eigvecs, ("blk", "grid"), axis=0, tiled=True)
    kzs = kernel(centers, sub_rows).astype(jnp.bfloat16)
    ksb_piece = kernel(sub_rows, batch).astype(jnp.bfloat16)
    kze_next = jnp.dot(kzs, vec_rows, preferred_element_type=jnp.float32)
    proj_next = lax.dot_general(
        vec_rows, ksb_piece, (((0,), (0,)), ((), ())), preferred_element_type=jnp.float32
    )
    coeff = jnp.dot(proj_next, resid.astype(jnp.float32), precision=lax.Precision.HIGHEST)
    scaled = scales[:, None] * coeff
    sub_increment = jnp.dot(eigvecs.astype(jnp.float32), scaled, precision=lax.Precision.HIGHEST)
    correction = jnp.dot(kze_next, scaled, precision=lax.Precision.HIGHEST)
    first = lax.dot_general(
        kbz, resid, (((0,), (0,)), ((), ())), preferred_element_type=jnp.float32
    )
    center_grad = (first - correction).astype(jnp.bfloat16)
    return (predictions, center_grad, sub_increment)


def solution(mesh):
    return jax.shard_map(
        local,
        mesh=mesh,
        in_specs=(
            P(("blk", "grid"), None),
            P(("blk", "grid"), None),
            P(),
            P(),
            P(("blk", "grid")),
            P(("blk", "grid"), None),
            P(),
        ),
        out_specs=(P(), P(("blk", "grid"), None), P(("blk", "grid"), None)),
        check_vma=False,
    )
```

profile of v0, /device:TPU:0, one launch (start us, length us, event | category | flops | bytes accessed | tf_op | source)
XLA Modules:
  0.0 215.3 jit_solution(7999707913510482286)
XLA Ops:
  7.2 0.0 copy-start
  7.2 0.0 all-reduce.3.cloned.1.call-start
  7.2 1.0 multiply_reduce_fusion.2
  8.3 0.7 compare_and_fusion.1
  9.0 0.0 copy-done
  9.0 2.0 gather_fusion
  11.0 0.2 convert_select_fusion
  11.2 0.0 copy-start.2
  11.2 53.3 %all-reduce.4 = bf16[512,512]{1,0:T(8,128)(2,1)S(1)} all-reduce(f32[512,512]{1,0:T(8,128)S(1)} %convert_select_fusion), channel_id=1, replica_groups=mesh['blk'=2,'grid'=16] {'blk','grid'}, use_global_device_ids=true, to_apply=%region_0.1 | all-reduce | flops 262144 | bytes 1572864 | tf_op jit(solution)/shard_map/psum | solution.py:34
  64.5 0.2 multiply_reduce_fusion
  64.6 0.3 fusion.17
  65.0 0.0 copy-done.2
  65.0 0.0 copy-start.6
  65.0 0.0 copy-start.3
  65.0 1.8 fusion.35
  66.8 0.0 all-reduce.3.cloned.1.call-update
  66.8 0.0 copy-done.6
  66.8 0.0 copy-start.4
  66.8 0.0 copy-start.5
  66.8 0.6 gather_fusion.1
  67.4 0.0 copy-done.3
  67.4 39.6 %all_gather.7 = bf16[256,160]{1,0:T(8,128)(2,1)S(1)} all-gather(bf16[8,160]{1,0:T(8,128)(2,1)S(1)} %copy-done.3), channel_id=1, replica_groups=mesh['blk'=2,'grid'=16] {'blk','grid'}, dimensions={0}, use_global_device_ids=true | all-gather | bytes 84480 | tf_op jit(solution)/shard_map/all_gather | solution.py:42
  107.0 0.1 broadcast_select_fusion
  107.1 37.3 %all_gather.6 = bf16[256,512]{1,0:T(8,128)(2,1)S(1)} all-gather(bf16[8,512]{1,0:T(8,128)(2,1)S(1)} %broadcast_select_fusion), channel_id=1, replica_groups=mesh['blk'=2,'grid'=16] {'blk','grid'}, dimensions={0}, use_global_device_ids=true | all-gather | bytes 270336 | tf_op jit(solution)/shard_map/all_gather | solution.py:41
  144.4 0.1 multiply_reduce_fusion.1
  144.5 0.4 fusion.27
  144.9 0.7 fusion.9
  145.6 54.2 %all-reduce.3.cloned.1.call-done = f32[512,1000]{0,1:T(8,128)} async-done(((f32[512,1000]{0,1:T(8,128)}), f32[512,1000]{0,1:T(8,128)}) %all-reduce.3.cloned.1.call-update) | async-done | bytes 2048016 | tf_op jit(solution)/shard_map/psum | solution.py:37
  199.8 0.0 copy-done.4
  199.8 0.0 copy-done.5
  199.8 0.0 copy-start.1
  199.8 3.6 %convolution_multiply_fusion = f32[160,1000]{1,0:T(8,128)S(1)} fusion(f32[512,160]{1,0:T(8,128)S(1)} %fusion.9, f32[160]{0:T(256)S(1)} %copy-done.5, f32[512,1000]{0,1:T(8,128)} %all-reduce.3.cloned.1.call-done, s32[512]{0:T(512)S(1)} %copy-done.4), kind=kOutput, calls=%fused_computation.4 | convolution fusion | flops 985248000 | bytes 3018368 | tf_op jit(solution)/shard_map/dot_general | solution.py:49
  203.4 0.9 convolution_bitcast_fusion
  204.4 1.8 fusion.57
  206.2 0.0 copy-done.1
  206.2 1.1 convert_element_type.50
  207.3 1.1 fusion.8
  (4 shorter events, 0.0 us)
Async XLA Ops:
  7.2 1.8 copy-start
  7.2 192.6 %all-reduce.3.cloned.1.call-start = ((), (), s32[]{:S(2)}) async-start(), calls=%async_computation | async-start | bytes 4096000 | tf_op jit(solution)/shard_map/psum | solution.py:37
  11.2 53.8 %copy-start.2 = (f32[128,1000]{0,1:T(8,128)S(1)}, f32[128,1000]{0,1:T(8,128)}, u32[]{:S(2)}) copy-start(f32[128,1000]{0,1:T(8,128)} %param.8) | copy-start | bytes 1536004
  65.0 1.8 copy-start.6
  65.0 2.4 %copy-start.3 = (bf16[8,160]{1,0:T(8,128)(2,1)S(1)}, bf16[8,160]{1,0:T(8,128)(2,1)}, u32[]{:S(2)}) copy-start(bf16[8,160]{1,0:T(8,128)(2,1)} %param.12) | copy-start | bytes 7684
  66.8 133.0 %copy-start.4 = (s32[512]{0:T(512)S(1)}, s32[512]{0:T(512)}, u32[]{:S(2)}) copy-start(s32[512]{0:T(512)} %param.10) | copy-start | bytes 6148
  66.8 133.0 %copy-start.5 = (f32[160]{0:T(256)S(1)}, f32[160]{0:T(256)}, u32[]{:S(2)}) copy-start(f32[160]{0:T(256)} %param.13) | copy-start | bytes 1924
  199.8 6.4 %copy-start.1 = (f32[512,1000]{0,1:T(8,128)S(1)}, f32[512,1000]{0,1:T(8,128)}, u32[]{:S(2)}) copy-start(f32[512,1000]{0,1:T(8,128)} %all-reduce.3.cloned.1.call-done) | copy-start | bytes 6144004
Sparse Core Ops, SparseCore 0:
  66.9 132.8 all-reduce.2
where the time goes:
time: 215 us
  blocking collectives  130 us (60%)
  waiting for transfers between devices  54.2 us (25%)
  between operations  14.2 us (7%)
  matrix products  10.6 us (5%)
  other arithmetic  3.42 us (2%)
  local copies, waits for them, and re-layouts  2.58 us (1%)
    psum x1, waiting for transfers between devices, local(): total = lax.psum(partial_out, ('blk', 'grid'))  54.2 us
    psum x1, blocking collectives, local(): batch = lax.psum(picked, ('blk', 'grid')).astype(jnp.bfloat16)  53.3 us
    all_gather x1, blocking collectives, local(): vec_rows = lax.all_gather(eigvecs, ('blk', 'grid'), axis=0, tiled=True)  39.6 us
    all_gather x1, blocking collectives, local(): sub_rows = lax.all_gather(subset_here, ('blk', 'grid'), axis=0, tiled=True)  37.3 us
  transfers between devices with their start and end apart: 1, of which 1 were waited for; matrix products, arithmetic and copies ran while one was open for 1% of the time, Pallas kernels for 0%

commit v1 on v0

--- a/solution.py
+++ b/solution.py
@@ -34,7 +34,8 @@
     batch = lax.psum(picked, ("blk", "grid")).astype(jnp.bfloat16)
     kbz = kernel(batch, centers).astype(jnp.bfloat16)
     partial_out = jnp.dot(kbz, weights.astype(jnp.bfloat16), preferred_element_type=jnp.float32)
-    total = lax.psum(partial_out, ("blk", "grid"))
+    half = lax.psum(partial_out, "blk")
+    total = lax.psum(half, "grid")
     predictions = total.astype(jnp.bfloat16)
     resid = (total - one_hot(labels, classes)).astype(jnp.bfloat16)
     subset_here = jnp.take(centers, sub_index, axis=0)

time: 215 us -> 245 us (1.14)
  waiting for transfers between devices: 54.2 us -> 81.6 us
    psum x1 -> x2, waiting for transfers between devices: 54.2 us -> 81.6 us  [the longest x1 60.4 us: local(): half = lax.psum(partial_out, 'blk')]
  transfers between devices with their start and end apart: 1 -> 2, of which waited for: 1 -> 2; matrix products, arithmetic and copies ran while one was open for 1% -> 1% of each run, Pallas kernels for 0% -> 0%
where the time goes in v1:
time: 245 us
  blocking collectives  132 us (54%)
  waiting for transfers between devices  81.6 us (33%)
  between operations  14.2 us (6%)
  matrix products  10.6 us (4%)
  other arithmetic  3.42 us (1%)
  local copies, waits for them, and re-layouts  2.58 us (1%)
    psum x1, waiting for transfers between devices, local(): half = lax.psum(partial_out, 'blk')  60.4 us
    psum x1, blocking collectives, local(): batch = lax.psum(picked, ('blk', 'grid')).astype(jnp.bfloat16)  53.3 us
    all_gather x1, blocking collectives, local(): vec_rows = lax.all_gather(eigvecs, ('blk', 'grid'), axis=0, tiled=True)  41.4 us
    all_gather x1, blocking collectives, local(): sub_rows = lax.all_gather(subset_here, ('blk', 'grid'), axis=0, tiled=True)  37.4 us
    psum x1, waiting for transfers between devices, local(): total = lax.psum(half, 'grid')  21.2 us
  transfers between devices with their start and end apart: 2, of which 2 were waited for; matrix products, arithmetic and copies ran while one was open for 1% of the time, Pallas kernels for 0%

profile of v1, /device:TPU:0, one launch (start us, length us, event | category | flops | bytes accessed | tf_op | source)
XLA Modules:
  0.0 244.6 jit_solution(3535265286102860149)
XLA Ops:
  7.2 0.0 copy-start
  7.2 0.0 all-reduce.4.cloned.1.call-start
  7.2 1.0 multiply_reduce_fusion.2
  8.3 0.7 compare_and_fusion.1
  9.0 0.0 copy-done
  9.0 2.0 gather_fusion
  11.0 0.2 convert_select_fusion
  11.2 0.0 copy-start.2
  11.2 53.3 %all-reduce.7 = bf16[512,512]{1,0:T(8,128)(2,1)S(1)} all-reduce(f32[512,512]{1,0:T(8,128)S(1)} %convert_select_fusion), channel_id=1, replica_groups=mesh['blk'=2,'grid'=16] {'blk','grid'}, use_global_device_ids=true, to_apply=%region_0.1 | all-reduce | flops 262144 | bytes 1572864 | tf_op jit(solution)/shard_map/psum | solution.py:34
  64.5 0.2 multiply_reduce_fusion
  64.6 0.3 fusion.17
  65.0 0.0 copy-done.2
  65.0 0.0 copy-start.6
  65.0 1.8 fusion.35
  66.7 0.0 copy-start.3
  66.7 0.0 all-reduce.4.cloned.1.call-update
  66.8 0.0 all-reduce.6.cloned.1.call-start
  66.8 0.0 copy-done.6
  66.9 60.4 %all-reduce.4.cloned.1.call-done = f32[512,1000]{0,1:T(8,128)} async-done(((f32[512,1000]{0,1:T(8,128)}), f32[512,1000]{0,1:T(8,128)}) %all-reduce.4.cloned.1.call-update) | async-done | bytes 2048016 | tf_op jit(solution)/shard_map/psum | solution.py:37
  127.3 0.0 all-reduce.6.cloned.1.call-update
  127.3 0.0 copy-start.4
  127.3 0.0 copy-start.5
  127.4 0.6 gather_fusion.1
  127.9 0.0 copy-done.3
  127.9 41.4 %all_gather.7 = bf16[256,160]{1,0:T(8,128)(2,1)S(1)} all-gather(bf16[8,160]{1,0:T(8,128)(2,1)S(1)} %copy-done.3), channel_id=1, replica_groups=mesh['blk'=2,'grid'=16] {'blk','grid'}, dimensions={0}, use_global_device_ids=true | all-gather | bytes 84480 | tf_op jit(solution)/shard_map/all_gather | solution.py:43
  169.3 0.1 broadcast_select_fusion
  169.4 37.4 %all_gather.6 = bf16[256,512]{1,0:T(8,128)(2,1)S(1)} all-gather(bf16[8,512]{1,0:T(8,128)(2,1)S(1)} %broadcast_select_fusion), channel_id=1, replica_groups=mesh['blk'=2,'grid'=16] {'blk','grid'}, dimensions={0}, use_global_device_ids=true | all-gather | bytes 270336 | tf_op jit(solution)/shard_map/all_gather | solution.py:42
  206.8 0.1 multiply_reduce_fusion.1
  206.9 0.4 fusion.27
  207.3 0.7 fusion.9
  208.0 21.2 %all-reduce.6.cloned.1.call-done = f32[512,1000]{0,1:T(8,128)} async-done(((f32[512,1000]{0,1:T(8,128)}), f32[512,1000]{0,1:T(8,128)}) %all-reduce.6.cloned.1.call-update) | async-done | bytes 2048016 | tf_op jit(solution)/shard_map/psum | solution.py:38
  229.2 0.0 copy-done.4
  229.2 0.0 copy-done.5
  229.2 0.0 copy-start.1
  229.2 3.6 %convolution_multiply_fusion = f32[160,1000]{1,0:T(8,128)S(1)} fusion(f32[512,160]{1,0:T(8,128)S(1)} %fusion.9, f32[160]{0:T(256)S(1)} %copy-done.5, f32[512,1000]{0,1:T(8,128)} %all-reduce.6.cloned.1.call-done, s32[512]{0:T(512)S(1)} %copy-done.4), kind=kOutput, calls=%fused_computation.4 | convolution fusion | flops 985248000 | bytes 3018368 | tf_op jit(solution)/shard_map/dot_general | solution.py:50
  232.8 0.9 convolution_bitcast_fusion
  233.7 1.8 fusion.57
  235.6 0.0 copy-done.1
  235.6 1.1 convert_element_type.50
  236.7 1.1 fusion.8
  (4 shorter events, 0.0 us)
Async XLA Ops:
  7.2 1.8 copy-start
  7.2 120.1 %all-reduce.4.cloned.1.call-start = ((), (), s32[]{:S(2)}) async-start(), calls=%async_computation | async-start | bytes 4096000 | tf_op jit(solution)/shard_map/psum | solution.py:37
  11.2 53.8 %copy-start.2 = (f32[128,1000]{0,1:T(8,128)S(1)}, f32[128,1000]{0,1:T(8,128)}, u32[]{:S(2)}) copy-start(f32[128,1000]{0,1:T(8,128)} %param.8) | copy-start | bytes 1536004
  65.0 1.8 copy-start.6
  66.7 61.2 %copy-start.3 = (bf16[8,160]{1,0:T(8,128)(2,1)S(1)}, bf16[8,160]{1,0:T(8,128)(2,1)}, u32[]{:S(2)}) copy-start(bf16[8,160]{1,0:T(8,128)(2,1)} %param.12) | copy-start | bytes 7684
  66.8 162.4 %all-reduce.6.cloned.1.call-start = ((), (), s32[]{:S(2)}) async-start(), calls=%async_computation.1 | async-start | bytes 4096000 | tf_op jit(solution)/shard_map/psum | solution.py:38
  127.3 101.9 %copy-start.4 = (s32[512]{0:T(512)S(1)}, s32[512]{0:T(512)}, u32[]{:S(2)}) copy-start(s32[512]{0:T(512)} %param.10) | copy-start | bytes 6148
  127.3 101.9 %copy-start.5 = (f32[160]{0:T(256)S(1)}, f32[160]{0:T(256)}, u32[]{:S(2)}) copy-start(f32[160]{0:T(256)} %param.13) | copy-start | bytes 1924
  229.2 6.4 %copy-start.1 = (f32[512,1000]{0,1:T(8,128)S(1)}, f32[512,1000]{0,1:T(8,128)}, u32[]{:S(2)}) copy-start(f32[512,1000]{0,1:T(8,128)} %all-reduce.6.cloned.1.call-done) | copy-start | bytes 6144004
Sparse Core Ops, SparseCore 0:
  66.9 60.3 all-reduce.3
  130.8 98.2 all-reduce.5
